TPU v7x, 32 devices: a whole 2x2x4 slice. The times are simulated.
32 devices in a mesh: group: 4 (over y, x), hash: 8 (over z, core).
Axes of the slice: x: 2, y: 2, z: 4, core: 2. Of those that a mesh axis runs over, the one named last changes fastest.
Arguments:
- pooled: bfloat16 [8, 512, 32, 256], P('hash', 'group'), may hold values from -0.375 to 0.375
- weight: bfloat16 [1024, 2048], replicated, may hold values from -0.1875 to 0.1875
- cotangent: bfloat16 [8, 512, 2048], P('hash', 'group'), may hold values from -6 to 6
- owners: int32 [8, 32, 512, 2], P('hash', 'group'), may hold values from 0 to 7, all different within a row; in each aligned block of 4096 rows (0 to 4095, 4096 to 8191, ..., all dimensions but the last counted through in order) at most 1365 rows name the same one
- local_rows: int32 [8, 32, 512, 2], P('hash', 'group'), may hold values from 0 to 511
- table: float32 [32, 4096, 256], P('group', 'hash'), may hold values from -0.625 to 0.625
- accum: float32 [32, 4096], P('group', 'hash'), may hold values from 0.05 to 2
Outputs:
- wgrad: bfloat16 [1024, 2048], replicated
- table_out: float32 [32, 4096, 256], P('group', 'hash')
- accum_out: float32 [32, 4096], P('group', 'hash')
Inputs may be any that keep to these rules, and one draw needn't show every extreme that they name: Among the rows of one device (aligned blocks of 4096 bags), no owner is named more than 1365 times, a bound that some block reaches; the 2 owners of one bag differ.
All inputs are finite; a program needn't handle non-finite values.
Results may differ from a plain program's by a relative error of at most 0.0059.
Values may be sent and summed in bfloat16 or wider, within the bound.
No kernel may reach another device: no remote copies, remote signals or barrier semaphores. Data moves between devices by JAX's collectives and lax.ppermute only.
A program may use at most 128 MiB of HBM per device.

v0:
```python
import math
import jax
import jax.numpy as jnp
from jax import lax
from jax.sharding import PartitionSpec as P


def local(pooled, weight, cotangent, owners, local_rows, table, accum):
    vectors = pooled[0]
    samples, feats, width = vectors.shape
    inter = jnp.einsum("sfe,sge->sfg", vectors, vectors, preferred_element_type=jnp.float32).astype(
        jnp.bfloat16
    )
    inter_rows = inter.reshape(samples, feats * feats)
    preact = jnp.dot(inter_rows, weight, preferred_element_type=jnp.float32)
    sigmoid_v = jax.nn.sigmoid(preact)
    dpre = (
        cotangent[0].astype(jnp.float32) * (sigmoid_v * (1.0 + preact * (1.0 - sigmoid_v)))
    ).astype(jnp.bfloat16)
    dinter = lax.dot_general(
        dpre, weight, (((1,), (1,)), ((), ())), preferred_element_type=jnp.float32
    ).reshape(samples, feats, feats)
    dsym = (dinter + jnp.swapaxes(dinter, 1, 2)).astype(jnp.bfloat16)
    dpooled = jnp.einsum("sfg,sge->fse", dsym, vectors, preferred_element_type=jnp.float32).astype(
        jnp.bfloat16
    )
    exchanged = lax.all_to_all(dpooled, "group", split_axis=0, concat_axis=1, tiled=True)
    wlocal = lax.dot_general(
        inter_rows, dpre, (((0,), (0,)), ((), ())), preferred_element_type=jnp.float32
    )
    total_samples = samples * lax.axis_size("group") * lax.axis_size("hash")
    wgrad = (lax.psum(wlocal, ("group", "hash")) / math.sqrt(total_samples)).astype(jnp.bfloat16)
    owner_ids = owners[0]
    row_ids = local_rows[0]
    groups_local, rows_dev = accum.shape
    hashes = lax.axis_size("hash")
    feature_index = jnp.arange(groups_local, dtype=jnp.int32)[:, None, None]
    values = jnp.broadcast_to(exchanged[:, :, None, :], owner_ids.shape + (width,)).reshape(
        -1, width
    )
    dense_keys = (feature_index * (hashes * rows_dev) + owner_ids * rows_dev + row_ids).reshape(-1)
    partial_grad = jax.ops.segment_sum(
        values.astype(jnp.float32), dense_keys, num_segments=groups_local * hashes * rows_dev
    )
    rowgrad = lax.psum_scatter(
        partial_grad.reshape(groups_local, hashes * rows_dev, width).astype(jnp.bfloat16),
        "hash",
        scatter_dimension=1,
        tiled=True,
    ).astype(jnp.float32)
    accum_out = accum + jnp.mean(rowgrad * rowgrad, axis=-1)
    table_out = table - 0.1 * rowgrad / jnp.sqrt(accum_out)[:, :, None]
    return (wgrad, table_out, accum_out)


def solution(mesh):
    in_specs = (
        P("hash", "group", None, None),
        P(),
        P("hash", "group", None),
        P("hash", "group", None, None),
        P("hash", "group", None, None),
        P("group", "hash", None),
        P("group", "hash"),
    )
    out_specs = (P(), P("group", "hash", None), P("group", "hash"))
    return jax.shard_map(local, mesh=mesh, in_specs=in_specs, out_specs=out_specs, check_vma=False)
```

profile of v0, /device:TPU:0, one launch (start us, length us, event | category | flops | bytes accessed | tf_op | source)
XLA Modules:
  0.0 382.3 jit_solution(6259762305518760065)
XLA Ops:
  8.0 0.0 copy-start
  8.0 0.0 all-reduce.2.cloned.1.call-start
  8.1 1.5 copy-done
  9.6 0.7 fusion.11
  10.3 1.1 copy.25
  11.4 0.0 copy-start.2
  11.4 3.0 fusion.27
  14.4 0.0 copy-done.2
  14.4 4.6 %fusion.17 = f32[1024,2048]{1,0:T(8,128)} fusion(bf16[128,1024]{0,1:T(8,128)(2,1)S(1)} %bitcast.47, f32[128,2048]{1,0:T(8,128)S(1)} %fusion.27, bf16[1,128,2048]{2,1,0:T(8,128)(2,1)S(1)} %copy-done.2), kind=kOutput, calls=%fused_computation.19 | convolution fusion | flops 539492352 | bytes 10223616 | tf_op jit(solution)/shard_map/dot_general | solution.py:28
  18.9 0.0 all-reduce.2.cloned.1.call-update
  19.0 3.7 fusion.15
  22.7 0.3 fusion.21
  23.0 1.4 copy.30
  24.5 0.7 convert_bitcast_fusion.1
  25.1 0.0 copy-start.4
  25.2 2.6 copy.31
  27.7 5.1 %all-to-all-start = ((bf16[32,128,256]{2,1,0:T(8,128)(2,1)}), bf16[32,128,256]{2,1,0:T(8,128)(2,1)S(1)}, u32[]{:S(2)}, u32[]{:S(2)}) async-start(bf16[32,128,256]{2,1,0:T(8,128)(2,1)} %copy.31), calls=%async_computation | async-start | bytes 4194304 | tf_op jit(solution)/shard_map/all_to_all | solution.py:27
  32.9 0.0 reduce-scatter.2.cloned.1.call-start
  32.9 0.0 copy-done.4
  32.9 0.0 copy-start.3
  32.9 2.0 copy.26
  34.9 3.1 mul.48
  38.0 1.5 add.47
  39.6 3.0 add.48
  42.6 0.0 copy-done.3
  42.6 2.0 copy.27
  44.6 3.0 squeeze.9
  47.7 20.9 %all-to-all-done = bf16[32,128,256]{2,1,0:T(8,128)(2,1)S(1)} async-done(((bf16[32,128,256]{2,1,0:T(8,128)(2,1)}), bf16[32,128,256]{2,1,0:T(8,128)(2,1)S(1)}, u32[]{:S(2)}, u32[]{:S(2)}) %all-to-all-start) | async-done | bytes 2097184 | tf_op jit(solution)/shard_map/all_to_all | solution.py:27
  68.6 0.5 convert_bitcast_fusion
  69.1 0.4 copy.32
  69.6 4.5 %broadcast_in_dim.5 = f32[8,512,2,256]{3,2,1,0:T(2,128)} broadcast(f32[8,512,256]{2,1,0:T(8,128)S(1)} %bitcast.44), dimensions={0,1,3} | broadcast | bytes 12582912 | tf_op jit(solution)/shard_map/broadcast_in_dim | solution.py:38
  74.0 11.1 %reshape.73 = f32[8192,256]{1,0:T(8,128)} reshape(f32[8,512,2,256]{3,2,1,0:T(2,128)} %broadcast_in_dim.5) | data formatting | bytes 16777216 | tf_op jit(solution)/shard_map/convert_element_type | solution.py:43
  85.2 58.1 %scatter_custom_fusion = f32[32768,256]{1,0:T(8,128)} fusion(s32[8192]{0:T(1024)S(1)} %bitcast.49, f32[8192,256]{1,0:T(8,128)} %reshape.73, f32[]{:T(128)} %constant.3.clone.1), kind=kCustom, calls=%fused_computation.1 | custom fusion | flops 2097152 | bytes 33554944 | tf_op jit(solution)/shard_map/scatter-add | solution.py:42
  143.3 17.5 %convert_element_type.62 = bf16[32768,256]{1,0:T(8,128)(2,1)} convert(f32[32768,256]{1,0:T(8,128)} %scatter_custom_fusion) | non-fusion elementwise | flops 8388608 | bytes 50331648 | tf_op jit(solution)/shard_map/convert_element_type | solution.py:46
  160.7 0.0 reduce-scatter.2.cloned.1.call-update
  160.8 0.0 copy-start.5
  160.8 115.0 %all-reduce.2.cloned.1.call-done = f32[1024,2048]{1,0:T(8,128)} async-done(((f32[1024,2048]{1,0:T(8,128)}), f32[1024,2048]{1,0:T(8,128)}) %all-reduce.2.cloned.1.call-update) | async-done | bytes 8388624 | tf_op jit(solution)/shard_map/psum | solution.py:32
  275.7 6.6 %multiply_convert_fusion = bf16[1024,2048]{1,0:T(8,128)(2,1)} fusion(f32[1024,2048]{1,0:T(8,128)} %all-reduce.2.cloned.1.call-done), kind=kLoop, calls=%fused_computation.3 | loop fusion | flops 4194304 | bytes 12582912 | tf_op jit(solution)/shard_map/convert_element_type | solution.py:32
  282.3 85.0 %reduce-scatter.2.cloned.1.call-done = bf16[8,512,256]{2,1,0:T(8,128)(2,1)} async-done(((bf16[8,4096,256]{2,1,0:T(8,128)(2,1)}), bf16[8,512,256]{2,1,0:T(8,128)(2,1)}) %reduce-scatter.2.cloned.1.call-update) | async-done | bytes 2097168 | tf_op jit(solution)/shard_map/reduce_scatter | solution.py:45
  367.4 2.2 fusion.4
  369.6 0.0 copy-done.5
  369.6 0.6 fusion.26
  370.2 0.0 copy-start.1
  370.2 4.6 %fusion.3 = f32[8,512,256]{2,1,0:T(8,128)} fusion(f32[8,512,256]{2,1,0:T(8,128)} %param.12, bf16[8,512,256]{2,1,0:T(8,128)(2,1)} %reduce-scatter.2.cloned.1.call-done, f32[8,512]{1,0:T(8,128)S(1)} %get-tuple-element.3), kind=kLoop, calls=%fused_computation.7 | loop fusion | flops 4194304 | bytes 10502144 | tf_op jit(solution)/shard_map/sub | solution.py:52
  374.8 0.0 copy-done.1
  (3 shorter events, 0.1 us)
Async XLA Ops:
  8.0 1.6 copy-start
  8.0 267.7 %all-reduce.2.cloned.1.call-start = ((), (), s32[]{:S(2)}) async-start(), calls=%async_computation.2 | async-start | bytes 16777216 | tf_op jit(solution)/shard_map/psum | solution.py:32
  11.4 3.0 copy-start.2
  25.1 7.7 %copy-start.4 = (s32[1,8,512,2]{2,3,1,0:T(2,128)S(1)}, s32[1,8,512,2]{2,3,1,0:T(2,128)}, u32[]{:S(2)}) copy-start(s32[1,8,512,2]{2,3,1,0:T(2,128)} %param.10) | copy-start | bytes 98308
  27.7 40.9 %all-to-all-start = ((bf16[32,128,256]{2,1,0:T(8,128)(2,1)}), bf16[32,128,256]{2,1,0:T(8,128)(2,1)S(1)}, u32[]{:S(2)}, u32[]{:S(2)}) async-start(bf16[32,128,256]{2,1,0:T(8,128)(2,1)} %copy.31), calls=%async_computation | async-start | bytes 4194304 | tf_op jit(solution)/shard_map/all_to_all | solution.py:27
  32.9 334.5 %reduce-scatter.2.cloned.1.call-start = ((), (), s32[]{:S(2)}) async-start(), calls=%async_computation.3 | async-start | bytes 18874368 | tf_op jit(solution)/shard_map/reduce_scatter | solution.py:45
  32.9 9.7 %copy-start.3 = (s32[1,8,512,2]{2,3,1,0:T(2,128)S(1)}, s32[1,8,512,2]{2,3,1,0:T(2,128)}, u32[]{:S(2)}) copy-start(s32[1,8,512,2]{2,3,1,0:T(2,128)} %param.11) | copy-start | bytes 98308
  160.8 208.8 %copy-start.5 = (f32[8,512]{1,0:T(8,128)S(1)}, f32[8,512]{1,0:T(8,128)}, u32[]{:S(2)}) copy-start(f32[8,512]{1,0:T(8,128)} %param.13) | copy-start | bytes 49156
  370.2 4.6 %copy-start.1 = (bf16[1,128,32,256]{3,2,1,0:T(8,128)(2,1)S(1)}, bf16[1,128,32,256]{3,2,1,0:T(8,128)(2,1)}, u32[]{:S(2)}) copy-start(bf16[1,128,32,256]{3,2,1,0:T(8,128)(2,1)} %param.7) | copy-start | bytes 6291460
Sparse Core Ops, SparseCore 0:
  19.1 256.6 all-reduce.1
Sparse Core Ops, SparseCore 1:
  160.8 206.5 reduce-scatter.1
where the time goes:
time: 383 us; the launch traced here: 382 us
  waiting for transfers between devices  221 us (58%)
  other arithmetic  90.5 us (24%)
  local copies, waits for them, and re-layouts  37.4 us (10%)
  between operations  15.6 us (4%)
  matrix products  12.6 us (3%)
  starting transfers between devices  5.15 us (1%)
    psum x1, waiting for transfers between devices, local(): lax.psum(wlocal, ('group', 'hash')) / math.sqrt(total_samples)  115 us
    reduce_scatter x1, waiting for transfers between devices, local(): lax.psum_scatter(partial_grad.reshape(groups_local, hashes * rows_dev, wi...  85 us
    scatter-add x1, other arithmetic, local(): jax.ops.segment_sum(values.astype(jnp.float32), dense_keys, num_segments=...  58.1 us
    all_to_all x1, waiting for transfers between devices, local(): lax.all_to_all(dpooled, 'group', split_axis=0, concat_axis=1, tiled=True)  20.9 us
    convert_element_type x1, other arithmetic, local(): partial_grad.reshape(groups_local, hashes * rows_dev, width)  17.5 us
    convert_element_type x2, local copies, waits for them, and re-layouts, local(): values.astype(jnp.float32)  11.6 us
  transfers between devices with their start and end apart: 3, of which 3 were waited for; matrix products, arithmetic and copies ran while one was open for 32% of the time, Pallas kernels for 0%

commit v1 on v0

--- a/solution.py
+++ b/solution.py
@@ -29,7 +29,8 @@
         inter_rows, dpre, (((0,), (0,)), ((), ())), preferred_element_type=jnp.float32
     )
     total_samples = samples * lax.axis_size("group") * lax.axis_size("hash")
-    wgrad = (lax.psum(wlocal, ("group", "hash")) / math.sqrt(total_samples)).astype(jnp.bfloat16)
+    apply_zones = lambda t0: lax.psum(lax.psum(t0, "hash"), "group")
+    wgrad = (apply_zones(wlocal) / math.sqrt(total_samples)).astype(jnp.bfloat16)
     owner_ids = owners[0]
     row_ids = local_rows[0]
     groups_local, rows_dev = accum.shape

time: 383 us -> 581 us (1.52)
  waiting for transfers between devices: 221 us -> 420 us
    psum x1 -> x2, waiting for transfers between devices: 115 us -> 222 us  [local(): apply_zones = lambda t0: lax.psum(lax.psum(t0, 'hash'), 'group')]
    reduce_scatter x1, waiting for transfers between devices: 85 us -> 165 us  [local(): lax.psum_scatter(partial_grad.reshape(groups_local, hashes * rows_dev, wi...]
    all_to_all x1, waiting for transfers between devices: 20.9 us -> 33.3 us  [local(): lax.all_to_all(dpooled, 'group', split_axis=0, concat_axis=1, tiled=True)]
  transfers between devices with their start and end apart: 3 -> 4, of which waited for: 3 -> 4; matrix products, arithmetic and copies ran while one was open for 32% -> 21% of each run, Pallas kernels for 0% -> 0%
where the time goes in v1:
time: 581 us; the launch traced here: 580 us
  waiting for transfers between devices  420 us (72%)
  other arithmetic  92 us (16%)
  local copies, waits for them, and re-layouts  37.1 us (6%)
  between operations  13.9 us (2%)
  matrix products  12.6 us (2%)
    psum x2, waiting for transfers between devices, local(): apply_zones = lambda t0: lax.psum(lax.psum(t0, 'hash'), 'group')  222 us
    reduce_scatter x1, waiting for transfers between devices, local(): lax.psum_scatter(partial_grad.reshape(groups_local, hashes * rows_dev, wi...  165 us
    scatter-add x1, other arithmetic, local(): jax.ops.segment_sum(values.astype(jnp.float32), dense_keys, num_segments=...  58.9 us
    all_to_all x1, waiting for transfers between devices, local(): lax.all_to_all(dpooled, 'group', split_axis=0, concat_axis=1, tiled=True)  33.3 us
    convert_element_type x1, other arithmetic, local(): partial_grad.reshape(groups_local, hashes * rows_dev, width)  18.2 us
  transfers between devices with their start and end apart: 4, of which 4 were waited for; matrix products, arithmetic and copies ran while one was open for 21% of the time, Pallas kernels for 0%

profile of v1, /device:TPU:0, one launch (start us, length us, event | category | flops | bytes accessed | tf_op | source)
XLA Modules:
  0.0 580.0 jit_solution(16090727430445273600)
XLA Ops:
  7.2 0.0 copy-start
  7.2 0.0 all-reduce.3.cloned.1.call-start
  7.2 1.5 copy-done
  8.8 0.7 fusion.11
  9.4 1.1 copy.25
  10.5 0.0 copy-start.2
  10.5 3.0 fusion.27
  13.5 0.0 copy-done.2
  13.5 4.6 fusion.17
  18.1 0.0 all-reduce.3.cloned.1.call-update
  18.1 0.0 all-reduce.5.cloned.1.call-start
  18.2 178.4 %all-reduce.3.cloned.1.call-done = f32[1024,2048]{1,0:T(8,128)} async-done(((f32[1024,2048]{1,0:T(8,128)}), f32[1024,2048]{1,0:T(8,128)}) %all-reduce.3.cloned.1.call-update) | async-done | bytes 8388624 | tf_op jit(solution)/shard_map/psum | solution.py:32
  196.5 0.0 all-reduce.5.cloned.1.call-update
  196.6 3.7 fusion.15
  200.3 0.3 fusion.21
  200.6 1.4 copy.30
  202.1 0.7 convert_bitcast_fusion.1
  202.7 0.0 copy-start.4
  202.8 2.5 copy.31
  205.3 3.6 all-to-all-start
  208.9 0.2 reduce-scatter.2.cloned.1.call-start
  209.1 0.0 copy-done.4
  209.1 0.0 copy-start.3
  209.2 2.0 copy.26
  211.1 3.0 mul.48
  214.2 1.5 add.49
  215.7 3.0 add.50
  218.8 0.0 copy-done.3
  218.8 2.0 copy.27
  220.7 3.0 squeeze.9
  223.9 33.3 %all-to-all-done = bf16[32,128,256]{2,1,0:T(8,128)(2,1)S(1)} async-done(((bf16[32,128,256]{2,1,0:T(8,128)(2,1)}), bf16[32,128,256]{2,1,0:T(8,128)(2,1)S(1)}, u32[]{:S(2)}, u32[]{:S(2)}) %all-to-all-start) | async-done | bytes 2097184 | tf_op jit(solution)/shard_map/all_to_all | solution.py:27
  257.2 0.5 convert_bitcast_fusion
  257.7 0.4 copy.32
  258.1 4.5 broadcast_in_dim.5
  262.6 10.9 %reshape.73 = f32[8192,256]{1,0:T(8,128)} reshape(f32[8,512,2,256]{3,2,1,0:T(2,128)} %broadcast_in_dim.5) | data formatting | bytes 16777216 | tf_op jit(solution)/shard_map/convert_element_type | solution.py:44
  273.5 58.9 %scatter_custom_fusion = f32[32768,256]{1,0:T(8,128)} fusion(s32[8192]{0:T(1024)S(1)} %bitcast.49, f32[8192,256]{1,0:T(8,128)} %reshape.73, f32[]{:T(128)} %constant.3.clone.1), kind=kCustom, calls=%fused_computation.1 | custom fusion | flops 2097152 | bytes 33554944 | tf_op jit(solution)/shard_map/scatter-add | solution.py:43
  332.4 18.2 %convert_element_type.62 = bf16[32768,256]{1,0:T(8,128)(2,1)} convert(f32[32768,256]{1,0:T(8,128)} %scatter_custom_fusion) | non-fusion elementwise | flops 8388608 | bytes 50331648 | tf_op jit(solution)/shard_map/convert_element_type | solution.py:47
  350.7 0.0 reduce-scatter.2.cloned.1.call-update
  350.7 0.0 copy-start.5
  350.7 44.0 %all-reduce.5.cloned.1.call-done = f32[1024,2048]{1,0:T(8,128)} async-done(((f32[1024,2048]{1,0:T(8,128)}), f32[1024,2048]{1,0:T(8,128)}) %all-reduce.5.cloned.1.call-update) | async-done | bytes 8388624 | tf_op jit(solution)/shard_map/psum | solution.py:32
  394.7 6.5 %multiply_convert_fusion = bf16[1024,2048]{1,0:T(8,128)(2,1)} fusion(f32[1024,2048]{1,0:T(8,128)} %all-reduce.5.cloned.1.call-done), kind=kLoop, calls=%fused_computation.3 | loop fusion | flops 4194304 | bytes 12582912 | tf_op jit(solution)/shard_map/convert_element_type | solution.py:33
  401.3 164.7 %reduce-scatter.2.cloned.1.call-done = bf16[8,512,256]{2,1,0:T(8,128)(2,1)} async-done(((bf16[8,4096,256]{2,1,0:T(8,128)(2,1)}), bf16[8,512,256]{2,1,0:T(8,128)(2,1)}) %reduce-scatter.2.cloned.1.call-update) | async-done | bytes 2097168 | tf_op jit(solution)/shard_map/reduce_scatter | solution.py:46
  566.0 2.2 fusion.4
  568.2 0.0 copy-done.5
  568.2 0.6 fusion.26
  568.8 0.0 copy-start.1
  568.8 4.6 fusion.3
  573.5 0.0 copy-done.1
  (3 shorter events, 0.1 us)
Async XLA Ops:
  7.2 1.6 copy-start
  7.2 189.4 %all-reduce.3.cloned.1.call-start = ((), (), s32[]{:S(2)}) async-start(), calls=%async_computation.2 | async-start | bytes 16777216 | tf_op jit(solution)/shard_map/psum | solution.py:32
  10.5 3.0 copy-start.2
  18.1 376.6 %all-reduce.5.cloned.1.call-start = ((), (), s32[]{:S(2)}) async-start(), calls=%async_computation.3 | async-start | bytes 16777216 | tf_op jit(solution)/shard_map/psum | solution.py:32
  202.7 6.4 %copy-start.4 = (s32[1,8,512,2]{2,3,1,0:T(2,128)S(1)}, s32[1,8,512,2]{2,3,1,0:T(2,128)}, u32[]{:S(2)}) copy-start(s32[1,8,512,2]{2,3,1,0:T(2,128)} %param.10) | copy-start | bytes 98308
  205.3 51.9 %all-to-all-start = ((bf16[32,128,256]{2,1,0:T(8,128)(2,1)}), bf16[32,128,256]{2,1,0:T(8,128)(2,1)S(1)}, u32[]{:S(2)}, u32[]{:S(2)}) async-start(bf16[32,128,256]{2,1,0:T(8,128)(2,1)} %copy.31), calls=%async_computation | async-start | bytes 4194304 | tf_op jit(solution)/shard_map/all_to_all | solution.py:27
  208.9 357.1 %reduce-scatter.2.cloned.1.call-start = ((), (), s32[]{:S(2)}) async-start(), calls=%async_computation.4 | async-start | bytes 18874368 | tf_op jit(solution)/shard_map/reduce_scatter | solution.py:46
  209.1 9.6 %copy-start.3 = (s32[1,8,512,2]{2,3,1,0:T(2,128)S(1)}, s32[1,8,512,2]{2,3,1,0:T(2,128)}, u32[]{:S(2)}) copy-start(s32[1,8,512,2]{2,3,1,0:T(2,128)} %param.11) | copy-start | bytes 98308
  350.7 217.5 %copy-start.5 = (f32[8,512]{1,0:T(8,128)S(1)}, f32[8,512]{1,0:T(8,128)}, u32[]{:S(2)}) copy-start(f32[8,512]{1,0:T(8,128)} %param.13) | copy-start | bytes 49156
  568.8 4.6 copy-start.1
Sparse Core Ops, SparseCore 0:
  18.3 178.2 all-reduce.2
  200.1 194.6 all-reduce.4
  397.1 168.8 reduce-scatter.1
